TPU v7x, 32 devices: a whole 2x2x4 slice. The times are simulated.
32 devices in a mesh: dp: 8 (over z, x), tensor: 4 (over y, core).
Axes of the slice: x: 2, y: 2, z: 4, core: 2. Of those that a mesh axis runs over, the one named last changes fastest.
Arguments:
- frames: bfloat16 [12288, 768], P(('dp', 'tensor')), may hold values from -6 to 6
- segments: int32 [8, 1536], P('dp'), may hold values from 0 to 15, never falling along the last dimension, each value on 1 to 768 neighbouring positions
- norm1_gain: float32 [768], P(('dp', 'tensor')), may hold values from 0.25 to 1.75
- norm1_shift: float32 [768], P(('dp', 'tensor')), may hold values from -1.5 to 1.5
- in_weight: bfloat16 [768, 3, 768], P('dp', None, 'tensor'), may hold values from -0.21875 to 0.21875
- proj_bias: bfloat16 [2, 12, 64], P(None, 'tensor', 'dp'), may hold values from -1.5 to 1.5
- out_weight: bfloat16 [768, 768], P('tensor', 'dp'), may hold values from -0.875 to 0.875
- out_bias: float32 [768], P(('dp', 'tensor')), may hold values from -1.5 to 1.5
- norm2_gain: float32 [768], P(('dp', 'tensor')), may hold values from 0.25 to 1.75
- norm2_shift: float32 [768], P(('dp', 'tensor')), may hold values from -1.5 to 1.5
- fc1_weight: bfloat16 [768, 3072], P('dp', 'tensor'), may hold values from -0.21875 to 0.21875
- fc1_bias: bfloat16 [48, 64], P('tensor', 'dp'), may hold values from -1.5 to 1.5
- fc2_weight: bfloat16 [3072, 768], P('tensor', 'dp'), may hold values from -0.109375 to 0.109375
- fc2_bias: float32 [768], P(('dp', 'tensor')), may hold values from -1.5 to 1.5
- cotangent: bfloat16 [12288, 768], P(('dp', 'tensor')), may hold values from -6 to 6
Outputs:
- output: bfloat16 [12288, 768], P(('dp', 'tensor'))
- grad_frames: float32 [12288, 768], P(('dp', 'tensor'))
- grad_norm1_gain: float32 [768], P(('dp', 'tensor'))
- grad_norm1_shift: float32 [768], P(('dp', 'tensor'))
- grad_in_weight: float32 [768, 3, 768], P('dp', None, 'tensor')
- grad_proj_bias: float32 [2, 12, 64], P(None, 'tensor', 'dp')
- grad_out_weight: float32 [768, 768], P('tensor', 'dp')
- grad_out_bias: float32 [768], P(('dp', 'tensor'))
- grad_norm2_gain: float32 [768], P(('dp', 'tensor'))
- grad_norm2_shift: float32 [768], P(('dp', 'tensor'))
- grad_fc1_weight: float32 [768, 3072], P('dp', 'tensor')
- grad_fc1_bias: float32 [48, 64], P('tensor', 'dp')
- grad_fc2_weight: float32 [3072, 768], P('tensor', 'dp')
- grad_fc2_bias: float32 [768], P(('dp', 'tensor'))
Inputs may be any that keep to these rules, and one draw needn't show every extreme that they name: `segments`: within each sequence the numbers never fall, every number appears, each covers 1 to 768 frames, and one covers exactly 768.
All inputs are finite; a program needn't handle non-finite values.
Results may differ from a plain program's by a relative error of at most 0.015.
Values may be sent and summed in bfloat16 or wider, within the bound.
A program may use at most 128 MiB of HBM per device.

v0:
```python
import jax
import jax.numpy as jnp
from jax import lax
from jax.sharding import PartitionSpec as P

HD = 64


def layer_norm(row_block, norm_gain, norm_shift):
    row_mean = jnp.mean(row_block, axis=-1, keepdims=True)
    centred = row_block - row_mean
    row_var = jnp.mean(centred * centred, axis=-1, keepdims=True)
    return centred * lax.rsqrt(row_var + 1e-05) * norm_gain + norm_shift


def gelu_exact(values_in):
    return jax.nn.gelu(values_in, approximate=False)


def contract(pattern, left, right):
    return jnp.einsum(pattern, left, right, preferred_element_type=jnp.float32)


def on_device(
    frames,
    segments,
    norm1_gain,
    norm1_shift,
    in_weight,
    proj_bias,
    out_weight,
    out_bias,
    norm2_gain,
    norm2_shift,
    fc1_weight,
    fc1_bias,
    fc2_weight,
    fc2_bias,
    cotangent,
):
    gain_one, shift_one, gain_two, shift_two, bias_out, bias_fc2 = (
        lax.all_gather(norm1_gain, ("dp", "tensor"), axis=0, tiled=True),
        lax.all_gather(norm1_shift, ("dp", "tensor"), axis=0, tiled=True),
        lax.all_gather(norm2_gain, ("dp", "tensor"), axis=0, tiled=True),
        lax.all_gather(norm2_shift, ("dp", "tensor"), axis=0, tiled=True),
        lax.all_gather(out_bias, ("dp", "tensor"), axis=0, tiled=True),
        lax.all_gather(fc2_bias, ("dp", "tensor"), axis=0, tiled=True),
    )
    in_full, proj_full, out_full, fc1_full, fc1b_full, fc2_full = (
        lax.all_gather(in_weight, "dp", axis=0, tiled=True),
        lax.all_gather(proj_bias, "dp", axis=2, tiled=True),
        lax.all_gather(out_weight, "dp", axis=1, tiled=True),
        lax.all_gather(fc1_weight, "dp", axis=0, tiled=True),
        lax.all_gather(fc1_bias, "dp", axis=1, tiled=True),
        lax.all_gather(fc2_weight, "dp", axis=1, tiled=True),
    )
    model_width = frames.shape[1]
    doc_ids = segments[0]
    seq_length = doc_ids.shape[0]
    heads_width = in_full.shape[2]
    local_heads = heads_width // HD
    block_rows = min(512, seq_length)
    num_blocks = seq_length // block_rows
    rows_in = frames.astype(jnp.float32)
    normed = layer_norm(rows_in, gain_one, shift_one).astype(jnp.bfloat16)
    normed_all = lax.all_gather(normed, "tensor", axis=0, tiled=True)
    projected = jnp.dot(
        normed_all,
        in_full.reshape(model_width, 3 * heads_width),
        preferred_element_type=jnp.float32,
    ).reshape(seq_length, 3, heads_width)
    bias_pair = proj_full.astype(jnp.float32).reshape(2, heads_width)
    query = (
        (projected[:, 0] + bias_pair[0]).astype(jnp.bfloat16).reshape(seq_length, local_heads, HD)
    )
    keys_all = projected[:, 1].astype(jnp.bfloat16).reshape(seq_length, local_heads, HD)
    values_all = (
        (projected[:, 2] + bias_pair[1]).astype(jnp.bfloat16).reshape(seq_length, local_heads, HD)
    )

    def scores_of(query_block, doc_block):
        raw_scores = contract("qhe,khe->hqk", query_block, keys_all) * 0.125
        same_doc = doc_block[:, None] == doc_ids[None, :]
        return jnp.where(same_doc[None], raw_scores, -1e30)

    def forward_block(block_index):
        block_start = block_index * block_rows
        query_block = lax.dynamic_slice_in_dim(query, block_start, block_rows, 0)
        doc_block = lax.dynamic_slice_in_dim(doc_ids, block_start, block_rows, 0)
        scores = scores_of(query_block, doc_block)
        row_max = jnp.max(scores, axis=-1, keepdims=True)
        exp_scores = jnp.exp(scores - row_max)
        row_total = jnp.sum(exp_scores, axis=-1, keepdims=True)
        attn_probs = (exp_scores / row_total).astype(jnp.bfloat16)
        block_mixed = contract("hqk,khe->qhe", attn_probs, values_all)
        log_total = (row_max + jnp.log(row_total))[..., 0]
        return (block_mixed.astype(jnp.bfloat16).reshape(block_rows, heads_width), log_total)

    mixed_blocks, log_totals = lax.map(forward_block, jnp.arange(num_blocks, dtype=jnp.int32))
    attn_mixed = mixed_blocks.reshape(seq_length, heads_width)
    attn_partial = jnp.dot(attn_mixed, out_full, preferred_element_type=jnp.float32)
    attended = lax.psum_scatter(attn_partial, "tensor", scatter_dimension=0, tiled=True) + bias_out
    middle = rows_in + attended
    normed_two = layer_norm(middle, gain_two, shift_two).astype(jnp.bfloat16)
    grad_out = cotangent.astype(jnp.float32)
    normed_two_all = lax.all_gather(normed_two, "tensor", axis=0, tiled=True)
    hidden = jnp.dot(
        normed_two_all, fc1_full, preferred_element_type=jnp.float32
    ) + fc1b_full.astype(jnp.float32).reshape(-1)
    active = gelu_exact(hidden).astype(jnp.bfloat16)
    branch = (
        lax.psum_scatter(
            jnp.dot(active, fc2_full, preferred_element_type=jnp.float32).astype(jnp.bfloat16),
            "tensor",
            scatter_dimension=0,
            tiled=True,
        ).astype(jnp.float32)
        + bias_fc2
    )
    output = (middle + branch).astype(jnp.bfloat16)
    grad_branch_all = lax.all_gather(cotangent, "tensor", axis=0, tiled=True)
    grad_fc2 = contract("lf,ld->fd", active, grad_branch_all)
    grad_active = contract("ld,fd->lf", grad_branch_all, fc2_full)
    grad_hidden = jax.vjp(gelu_exact, hidden)[1](grad_active)[0].astype(jnp.bfloat16)
    grad_fc1 = contract("ld,lf->df", normed_two_all, grad_hidden)
    grad_fc1b = jnp.sum(grad_hidden.astype(jnp.float32), axis=0).reshape(fc1b_full.shape)
    grad_normed_two = lax.psum_scatter(
        contract("lf,df->ld", grad_hidden, fc1_full).astype(jnp.bfloat16),
        "tensor",
        scatter_dimension=0,
        tiled=True,
    ).astype(jnp.float32)
    grad_bias_fc2 = jnp.sum(grad_out, axis=0)
    norm_back_two = jax.vjp(layer_norm, middle, gain_two, shift_two)[1]
    grad_mid_norm, grad_gain_two, grad_shift_two = norm_back_two(grad_normed_two)
    grad_middle = grad_out + grad_mid_norm
    grad_attended = grad_middle.astype(jnp.bfloat16)
    grad_bias_out = jnp.sum(grad_attended.astype(jnp.float32), axis=0)
    grad_att_all = lax.all_gather(grad_attended, "tensor", axis=0, tiled=True)
    grad_out_w = contract("lh,ld->hd", attn_mixed, grad_att_all)
    grad_mixed = (
        contract("ld,hd->lh", grad_att_all, out_full)
        .astype(jnp.bfloat16)
        .reshape(seq_length, local_heads, HD)
    )

    def backward_block(carried, block_index):
        grad_keys_acc, grad_values_acc = carried
        block_start = block_index * block_rows
        query_block = lax.dynamic_slice_in_dim(query, block_start, block_rows, 0)
        doc_block = lax.dynamic_slice_in_dim(doc_ids, block_start, block_rows, 0)
        grad_block = lax.dynamic_slice_in_dim(grad_mixed, block_start, block_rows, 0)
        scores = scores_of(query_block, doc_block)
        attn_probs = jnp.exp(scores - log_totals[block_index][..., None])
        grad_probs = contract("qhe,khe->hqk", grad_block, values_all)
        row_inner = jnp.sum(attn_probs * grad_probs, axis=-1, keepdims=True)
        grad_scores = (attn_probs * (grad_probs - row_inner)).astype(jnp.bfloat16)
        grad_query_block = contract("hqk,khe->qhe", grad_scores, keys_all) * 0.125
        grad_keys_acc = grad_keys_acc + contract("hqk,qhe->khe", grad_scores, query_block) * 0.125
        grad_values_acc = grad_values_acc + contract(
            "hqk,qhe->khe", attn_probs.astype(jnp.bfloat16), grad_block
        )
        return ((grad_keys_acc, grad_values_acc), grad_query_block)

    empty_acc = jnp.zeros((seq_length, local_heads, HD), jnp.float32)
    (grad_keys_all, grad_values_all), grad_query_blocks = lax.scan(
        backward_block, (empty_acc, empty_acc), jnp.arange(num_blocks, dtype=jnp.int32)
    )
    grad_proj = jnp.stack(
        [
            grad_query_blocks.reshape(seq_length, heads_width),
            grad_keys_all.reshape(seq_length, heads_width),
            grad_values_all.reshape(seq_length, heads_width),
        ],
        axis=1,
    ).astype(jnp.bfloat16)
    grad_proj_sums = jnp.sum(grad_proj.astype(jnp.float32), axis=0)
    grad_proj_b = jnp.stack([grad_proj_sums[0], grad_proj_sums[2]], axis=0).reshape(
        2, local_heads, HD
    )
    grad_in_w = contract("ld,lcf->dcf", normed_all, grad_proj)
    grad_normed = lax.psum_scatter(
        contract("lcf,dcf->ld", grad_proj, in_full).astype(jnp.bfloat16),
        "tensor",
        scatter_dimension=0,
        tiled=True,
    ).astype(jnp.float32)
    norm_back_one = jax.vjp(layer_norm, rows_in, gain_one, shift_one)[1]
    grad_rows_norm, grad_gain_one, grad_shift_one = norm_back_one(grad_normed)
    grad_frames = grad_middle + grad_rows_norm
    g_in, g_proj, g_out, g_fc1, g_fc1b, g_fc2 = (
        lax.psum_scatter(grad_in_w, "dp", scatter_dimension=0, tiled=True),
        lax.psum_scatter(grad_proj_b, "dp", scatter_dimension=2, tiled=True),
        lax.psum_scatter(grad_out_w, "dp", scatter_dimension=1, tiled=True),
        lax.psum_scatter(grad_fc1, "dp", scatter_dimension=0, tiled=True),
        lax.psum_scatter(grad_fc1b, "dp", scatter_dimension=1, tiled=True),
        lax.psum_scatter(grad_fc2, "dp", scatter_dimension=1, tiled=True),
    )
    v_gain_one, v_shift_one, v_gain_two, v_shift_two, v_bias_out, v_bias_fc2 = (
        lax.psum_scatter(grad_gain_one, ("dp", "tensor"), scatter_dimension=0, tiled=True),
        lax.psum_scatter(grad_shift_one, ("dp", "tensor"), scatter_dimension=0, tiled=True),
        lax.psum_scatter(grad_gain_two, ("dp", "tensor"), scatter_dimension=0, tiled=True),
        lax.psum_scatter(grad_shift_two, ("dp", "tensor"), scatter_dimension=0, tiled=True),
        lax.psum_scatter(grad_bias_out, ("dp", "tensor"), scatter_dimension=0, tiled=True),
        lax.psum_scatter(grad_bias_fc2, ("dp", "tensor"), scatter_dimension=0, tiled=True),
    )
    return (
        output,
        grad_frames,
        v_gain_one,
        v_shift_one,
        g_in,
        g_proj,
        g_out,
        v_bias_out,
        v_gain_two,
        v_shift_two,
        g_fc1,
        g_fc1b,
        g_fc2,
        v_bias_fc2,
    )


def solution(mesh):
    in_specs = (
        P(("dp", "tensor"), None),
        P("dp", None),
        P(("dp", "tensor")),
        P(("dp", "tensor")),
        P("dp", None, "tensor"),
        P(None, "tensor", "dp"),
        P("tensor", "dp"),
        P(("dp", "tensor")),
        P(("dp", "tensor")),
        P(("dp", "tensor")),
        P("dp", "tensor"),
        P("tensor", "dp"),
        P("tensor", "dp"),
        P(("dp", "tensor")),
        P(("dp", "tensor"), None),
    )
    out_specs = (
        P(("dp", "tensor"), None),
        P(("dp", "tensor"), None),
        P(("dp", "tensor")),
        P(("dp", "tensor")),
        P("dp", None, "tensor"),
        P(None, "tensor", "dp"),
        P("tensor", "dp"),
        P(("dp", "tensor")),
        P(("dp", "tensor")),
        P(("dp", "tensor")),
        P("dp", "tensor"),
        P("tensor", "dp"),
        P("tensor", "dp"),
        P(("dp", "tensor")),
    )
    return jax.shard_map(
        on_device, mesh=mesh, in_specs=in_specs, out_specs=out_specs, check_vma=False
    )
```

profile of v0, /device:TPU:0, one launch (start us, length us, event | category | flops | bytes accessed | tf_op | source)
XLA Modules:
  0.0 845.4 jit_solution(4965968082217313966)
XLA Ops:
  15.0 42.3 %all-reduce.15 = (f32[768]{0:T(1024)S(1)}, f32[768]{0:T(1024)S(1)}, f32[768]{0:T(1024)S(1)}, f32[768]{0:T(1024)S(1)}, f32[768]{0:T(1024)S(1)}) all-reduce(f32[768]{0:T(1024)S(1)} %dynamic-update-slice.1, f32[768]{0:T(1024)S(1)} %dynamic-update-slice, f32[768]{0:T(1024)S(1)} %dynamic-update-slice.2, ...), channel_id=1, replica_groups=mesh['dp'=8,'tensor'=4] {'dp','tensor'}, use_global_device_ids=true, to_apply=%add.1 | all-reduce | flops 3840 | bytes 30720
  57.3 2.2 fusion.49
  59.8 30.4 %all_gather.52 = bf16[2,3,64]{1,0,2:T(2,128)(2,1)S(1)} all-gather(bf16[2,3,8]{1,0,2:T(2,128)(2,1)S(1)} %copy.61), channel_id=1, replica_groups=mesh['dp'=8,'tensor'=4] {'dp'}, dimensions={2}, use_global_device_ids=true | all-gather | bytes 864 | tf_op jit(solution)/shard_map/all_gather | solution.py:51
  90.5 33.8 %all_gather.51 = bf16[768,3,192]{2,0,1:T(8,128)(2,1)S(1)} all-gather(bf16[96,3,192]{2,0,1:T(8,128)(2,1)S(1)} %copy-done.26), channel_id=1, replica_groups=mesh['dp'=8,'tensor'=4] {'dp'}, dimensions={0}, use_global_device_ids=true | all-gather | bytes 995328 | tf_op jit(solution)/shard_map/all_gather | solution.py:50
  125.0 31.0 %all_gather.53 = bf16[192,768]{0,1:T(8,128)(2,1)S(1)} all-gather(bf16[192,96]{0,1:T(8,128)(2,1)S(1)} %copy.65), channel_id=1, replica_groups=mesh['dp'=8,'tensor'=4] {'dp'}, dimensions={1}, use_global_device_ids=true | all-gather | bytes 331776 | tf_op jit(solution)/shard_map/all_gather | solution.py:52
  155.9 3.4 fusion.38
  159.8 34.5 %while.27 = (s32[]{:T(128)}, bf16[3,512,192]{1,2,0:T(8,128)(2,1)}, f32[3,3,512]{2,1,0:T(4,128)}, s32[3]{0:T(128)S(1)}, s32[1536]{0:T(1024)S(1)}, /*index=5*/s32[...) while((s32[]{:T(128)}, bf16[3,512,192]{1,2,0:T(8,128)(2,1)}, ...), condition=%wide.region_5.6_spmd, body=%wide.region_2.5_spmd.sunk | while | flops 633174528 | bytes 33499348 | solution.py:99
  161.6 2.0 fusion.117
  163.6 2.8 fusion.118
  166.4 3.5 fusion.119
  173.1 2.0 fusion.117
  175.1 2.8 fusion.118
  177.9 3.5 fusion.119
  184.6 2.0 fusion.117
  186.6 2.8 fusion.118
  189.4 3.5 fusion.119
  195.6 3.0 fusion.67
  199.3 46.7 %reduce-scatter.13.cloned.1.call-done = f32[384,768]{1,0:T(8,128)} async-done(((f32[1536,768]{1,0:T(8,128)}), f32[384,768]{1,0:T(8,128)}) %reduce-scatter.13.cloned.1.call-update) | async-done | bytes 1179664 | tf_op jit(solution)/shard_map/reduce_scatter | solution.py:102
  250.3 26.5 %all_gather.59 = bf16[12,64]{0,1:T(8,128)(2,1)S(1)} all-gather(bf16[12,8]{0,1:T(8,128)(2,1)S(1)} %copy-done.41), channel_id=1, replica_groups=mesh['dp'=8,'tensor'=4] {'dp'}, dimensions={1}, use_global_device_ids=true | all-gather | bytes 1728 | tf_op jit(solution)/shard_map/all_gather | solution.py:54
  277.0 6.2 fusion.68
  283.1 33.6 %all-gather.13.cloned.1.call-done = bf16[768,768]{0,1:T(8,128)(2,1)} async-done(((bf16[768,96]{0,1:T(8,128)(2,1)}), bf16[768,768]{0,1:T(8,128)(2,1)}) %all-gather.13.cloned.1.call-update) | async-done | bytes 1179664 | tf_op jit(solution)/shard_map/all_gather | solution.py:55
  316.8 24.1 %all-gather.15.cloned.1.call-done = bf16[1536,768]{1,0:T(8,128)(2,1)} async-done(((bf16[384,768]{1,0:T(8,128)(2,1)}), bf16[1536,768]{1,0:T(8,128)(2,1)}) %all-gather.15.cloned.1.call-update) | async-done | bytes 2359312 | tf_op jit(solution)/shard_map/all_gather | solution.py:121
  340.9 16.0 %convert_reduce_fusion = (f32[768]{0:T(1024)}, bf16[1536,768]{1,0:T(8,128)(2,1)S(1)}, f32[1536,768]{1,0:T(8,128)}) fusion(f32[1536,768]{1,0:T(8,128)} %fusion.68, f32[768]{0:T(1024)S(1)} %reshape.224, bf16[1536,768]{1,0:T(8,128)(2,1)} %all-gather.15.cloned.1.call-done, bf16[768,768]{0,1:T(8,128)(2,1)} %all-gather.13.cloned.1.call-done), kind=kOutput, calls=%fused_computation.42 | convolution fusion | flops 1900412160 | bytes 15341568 | tf_op jit(solution)/shard_map/ld,fd->lf/dot_general | solution.py:21
  358.3 3.6 convolution_convert_fusion
  361.9 33.0 %reduce-scatter.17.cloned.1.call-done = bf16[384,768]{1,0:T(8,128)(2,1)} async-done(((bf16[1536,768]{1,0:T(8,128)(2,1)}), bf16[384,768]{1,0:T(8,128)(2,1)}) %reduce-scatter.17.cloned.1.call-update) | async-done | bytes 589840 | tf_op jit(solution)/shard_map/reduce_scatter | solution.py:127
  395.0 2.2 fusion.53
  399.8 1.7 convert_reduce_fusion.6
  401.6 24.1 %all-gather.17.cloned.1.call-done = bf16[1536,768]{1,0:T(8,128)(2,1)} async-done(((bf16[384,768]{1,0:T(8,128)(2,1)}), bf16[1536,768]{1,0:T(8,128)(2,1)}) %all-gather.17.cloned.1.call-update) | async-done | bytes 2359312 | tf_op jit(solution)/shard_map/all_gather | solution.py:139
  425.7 3.8 convolution_bitcast_fusion
  429.7 3.5 convolution_convert_fusion.2
  433.2 106.5 %while.28 = (s32[]{:T(128)}, f32[1536,3,64]{0,2,1:T(8,128)}, f32[1536,3,64]{0,2,1:T(8,128)S(1)}, bf16[3,512,3,64]{1,3,2,0:T(8,128)(2,1)}, s32[3]{0:T(128)S(1)}, ...) while((s32[]{:T(128)}, f32[1536,3,64]{0,2,1:T(8,128)}, ...), condition=%wide.region_15.16_spmd.clone, body=%wide.region_13.15_spmd.clone.sunk | while | flops 1533540864 | bytes 150903440 | solution.py:166
  439.7 2.3 fusion.129
  442.0 7.2 multiply_reduce_fusion.3
  449.2 9.5 %multiply_convert_fusion.3 = bf16[3,512,1536]{2,1,0:T(8,128)(2,1)} fusion(f32[3,512,1536]{2,1,0:T(8,128)} %get-tuple-element.446, f32[3,512,1536]{2,1,0:T(8,128)} %copy-done, f32[3,512]{1,0:T(4,128)S(1)} %get-tuple-element.447), kind=kLoop, calls=%fused_computation.15.clone.1 | loop fusion | flops 7077888 | bytes 23599104 | tf_op jit(solution)/shard_map/while/body/eval_jaxpr/convert_element_type | solution.py:157
  458.7 5.0 fusion.131
  465.6 2.1 fusion.130
  475.2 2.4 fusion.129
  477.6 7.2 multiply_reduce_fusion.3
  484.8 9.4 %multiply_convert_fusion.3 = bf16[3,512,1536]{2,1,0:T(8,128)(2,1)} fusion(f32[3,512,1536]{2,1,0:T(8,128)} %get-tuple-element.446, f32[3,512,1536]{2,1,0:T(8,128)} %copy-done, f32[3,512]{1,0:T(4,128)S(1)} %get-tuple-element.447), kind=kLoop, calls=%fused_computation.15.clone.1 | loop fusion | flops 7077888 | bytes 23599104 | tf_op jit(solution)/shard_map/while/body/eval_jaxpr/convert_element_type | solution.py:157
  494.2 5.0 fusion.131
  501.1 2.1 fusion.130
  510.7 2.4 fusion.129
  513.1 7.2 multiply_reduce_fusion.3
  520.3 9.4 %multiply_convert_fusion.3 = bf16[3,512,1536]{2,1,0:T(8,128)(2,1)} fusion(f32[3,512,1536]{2,1,0:T(8,128)} %get-tuple-element.446, f32[3,512,1536]{2,1,0:T(8,128)} %copy-done, f32[3,512]{1,0:T(4,128)S(1)} %get-tuple-element.447), kind=kLoop, calls=%fused_computation.15.clone.1 | loop fusion | flops 7077888 | bytes 23599104 | tf_op jit(solution)/shard_map/while/body/eval_jaxpr/convert_element_type | solution.py:157
  529.7 5.0 fusion.131
  536.5 2.1 fusion.130
  539.7 2.5 copy.67
  542.1 2.6 stack_reshape.12
  547.1 3.6 bitcast_convert_fusion
  551.5 4.5 multiply_convert_fusion.1
  557.4 3.5 convolution_convert_fusion.1
  560.9 5.8 fusion.70
  566.8 6.3 fusion.69
  574.5 5.2 fusion.36
  586.8 37.1 %all-reduce.16 = (f32[2,3,64]{2,1,0:T(4,128)S(1)}, f32[12,64]{1,0:T(8,128)S(1)}) all-reduce(f32[2,3,64]{2,1,0:T(4,128)S(1)} %reshape.222, f32[12,64]{1,0:T(8,128)} %reshape.223), channel_id=9, replica_groups=mesh['dp'=8,'tensor'=4] {'dp'}, use_global_device_ids=true, to_apply=%region_25.26.clone | all-reduce | flops 1152 | bytes 9216
  625.3 1.6 copy.76
  626.9 2.1 convert_reduce_fusion.2
  629.7 2.4 fusion.54
  632.1 3.3 add_add_fusion.2
  635.4 38.0 %all-reduce.14 = (f32[768]{0:T(1024)S(1)}, f32[768]{0:T(1024)S(1)}, f32[768]{0:T(1024)S(1)}, f32[768]{0:T(1024)S(1)}, f32[768]{0:T(1024)S(1)}, /*index=5*/f32[768]{0:T(1024)S(1)}, f32[768]{0:T(1024)S(1)}) all-reduce(f32[768]{0:T(1024)} %dynamic-update-slice.5, ...), channel_id=1, replica_groups=mesh['dp'=8,'tensor'=4] {'dp','tensor'}, use_global_device_ids=true, to_apply=%add.5 | all-reduce | flops 5376 | bytes 43008
  676.9 2.0 add_convert_fusion.1
  678.9 14.2 %reduce-scatter.25.cloned.1.call-done = f32[768,96]{0,1:T(8,128)} async-done(((f32[768,768]{0,1:T(8,128)}), f32[768,96]{0,1:T(8,128)}) %reduce-scatter.25.cloned.1.call-update) | async-done | bytes 294928 | tf_op jit(solution)/shard_map/reduce_scatter | solution.py:197
  693.1 72.5 %reduce-scatter.23.cloned.1.call-done = f32[96,768]{1,0:T(8,128)} async-done(((f32[768,768]{1,0:T(8,128)}), f32[96,768]{1,0:T(8,128)}) %reduce-scatter.23.cloned.1.call-update) | async-done | bytes 294928 | tf_op jit(solution)/shard_map/reduce_scatter | solution.py:195
  765.5 72.3 %reduce-scatter.21.cloned.1.call-done = f32[96,3,192]{2,0,1:T(8,128)} async-done(((f32[768,3,192]{2,0,1:T(8,128)}), f32[96,3,192]{2,0,1:T(8,128)}) %reduce-scatter.21.cloned.1.call-update) | async-done | bytes 221200 | tf_op jit(solution)/shard_map/reduce_scatter | solution.py:192
  (268 shorter events, 64.5 us)
Async XLA Ops:
  8.0 51.6 %copy-start.42 = (bf16[2,3,8]{2,0,1:T(2,128)(2,1)S(1)}, bf16[2,3,8]{2,0,1:T(2,128)(2,1)}, u32[]{:S(2)}) copy-start(bf16[2,3,8]{2,0,1:T(2,128)(2,1)} %param.24) | copy-start | bytes 292
  8.0 51.7 %copy-start.23 = (s32[1,1536]{1,0:T(1,128)S(1)}, s32[1,1536]{1,0:T(1,128)}, u32[]{:S(2)}) copy-start(s32[1,1536]{1,0:T(1,128)} %param.20) | copy-start | bytes 18436
  8.0 82.3 %copy-start.33 = (bf16[192,96]{1,0:T(8,128)(2,1)S(1)}, bf16[192,96]{1,0:T(8,128)(2,1)}, u32[]{:S(2)}) copy-start(bf16[192,96]{1,0:T(8,128)(2,1)} %param.25) | copy-start | bytes 110596
  8.0 82.4 %copy-start.26 = (bf16[96,3,192]{2,0,1:T(8,128)(2,1)S(1)}, bf16[96,3,192]{2,0,1:T(8,128)(2,1)}, u32[]{:S(2)}) copy-start(bf16[96,3,192]{2,0,1:T(8,128)(2,1)} %param.23) | copy-start | bytes 331780
  8.1 147.9 %all-gather.7.cloned.1.call-start = ((), (), s32[]{:S(2)}) async-start(), calls=%async_computation.8 | async-start | bytes 2949120 | tf_op jit(solution)/shard_map/all_gather | solution.py:66
  9.4 50.4 %copy-start.29 = (f32[384]{0:T(512)}, f32[384]{0:T(512)S(1)}, u32[]{:S(2)}) copy-start(f32[384]{0:T(512)S(1)} %broadcast_multiply_fusion.1) | copy-start | bytes 4612
  10.7 3.4 copy-start.38
  10.8 49.0 %copy-start.34 = (f32[384]{0:T(512)}, f32[384]{0:T(512)S(1)}, u32[]{:S(2)}) copy-start(f32[384]{0:T(512)S(1)} %fusion.58) | copy-start | bytes 4612
  57.3 2.4 copy-start.31
  59.5 186.5 %reduce-scatter.13.cloned.1.call-start = ((), (), s32[]{:S(2)}) async-start(), calls=%async_computation.9 | async-start | bytes 5898240 | tf_op jit(solution)/shard_map/reduce_scatter | solution.py:102
  124.3 35.0 %copy-start.11 = (bf16[768,3,192]{2,0,1:T(8,128)(2,1)}, bf16[768,3,192]{2,0,1:T(8,128)(2,1)S(1)}, u32[]{:S(2)}) copy-start(bf16[768,3,192]{2,0,1:T(8,128)(2,1)S(1)} %all_gather.51) | copy-start | bytes 2654212
  155.9 39.7 %copy-start.13 = (bf16[192,768]{0,1:T(8,128)(2,1)}, bf16[192,768]{0,1:T(8,128)(2,1)S(1)}, u32[]{:S(2)}) copy-start(bf16[192,768]{0,1:T(8,128)(2,1)S(1)} %all_gather.53) | copy-start | bytes 884740
  194.3 4.3 copy-start.6
  195.6 3.0 copy-start.21
  198.6 47.4 %copy-start.4 = (bf16[384,768]{1,0:T(8,128)(2,1)S(1)}, bf16[384,768]{1,0:T(8,128)(2,1)}, u32[]{:S(2)}) copy-start(bf16[384,768]{1,0:T(8,128)(2,1)} %param.19) | copy-start | bytes 1769476
  198.6 78.3 %all-gather.11.cloned.1.call-start = ((), (), s32[]{:S(2)}) async-start(), calls=%async_computation.11 | async-start | bytes 1327104 | tf_op jit(solution)/shard_map/all_gather | solution.py:53
  199.2 77.8 %all-gather.9.cloned.1.call-start = ((), (), s32[]{:S(2)}) async-start(), calls=%async_computation.10 | async-start | bytes 2949120 | tf_op jit(solution)/shard_map/all_gather | solution.py:106
  247.5 2.8 copy-start.41
  248.9 67.9 %all-gather.13.cloned.1.call-start = ((), (), s32[]{:S(2)}) async-start(), calls=%async_computation.12 | async-start | bytes 1327104 | tf_op jit(solution)/shard_map/all_gather | solution.py:55
  249.5 91.4 %all-gather.15.cloned.1.call-start = ((), (), s32[]{:S(2)}) async-start(), calls=%async_computation.14 | async-start | bytes 2949120 | tf_op jit(solution)/shard_map/all_gather | solution.py:121
  250.2 144.8 %reduce-scatter.17.cloned.1.call-start = ((), (), s32[]{:S(2)}) async-start(), calls=%async_computation.15 | async-start | bytes 2949120 | tf_op jit(solution)/shard_map/reduce_scatter | solution.py:127
  276.9 63.9 %copy-start.39 = (f32[768]{0:T(1024)}, f32[768]{0:T(1024)S(1)}, u32[]{:S(2)}) copy-start(f32[768]{0:T(1024)S(1)} %reshape.224) | copy-start | bytes 9220
  340.9 17.4 %copy-start.44 = (bf16[768,768]{1,0:T(8,128)(2,1)S(1)}, bf16[768,768]{1,0:T(8,128)(2,1)}, u32[]{:S(2)}) copy-start(bf16[768,768]{1,0:T(8,128)(2,1)} %all-gather.11.cloned.1.call-done) | copy-start | bytes 3538948
  361.9 37.9 %copy-start.10 = (bf16[384,768]{1,0:T(8,128)(2,1)S(1)}, bf16[384,768]{1,0:T(8,128)(2,1)}, u32[]{:S(2)}) copy-start(bf16[384,768]{1,0:T(8,128)(2,1)} %param.33) | copy-start | bytes 1769476
  361.9 63.8 %all-gather.17.cloned.1.call-start = ((), (), s32[]{:S(2)}) async-start(), calls=%async_computation.16 | async-start | bytes 2949120 | tf_op jit(solution)/shard_map/all_gather | solution.py:139
  398.7 2.8 copy-start.36
  401.5 223.8 %reduce-scatter.27.cloned.1.call-start = ((), (), s32[]{:S(2)}) async-start(), calls=%async_computation.21 | async-start | bytes 884736
  429.5 197.4 %reduce-scatter.19.cloned.1.call-start = ((), (), s32[]{:S(2)}) async-start(), calls=%async_computation.17 | async-start | bytes 2949120 | tf_op jit(solution)/shard_map/reduce_scatter | solution.py:182
  433.2 3.2 copy-start.45
  433.2 3.8 copy-start.27
  442.0 7.2 copy-start
  458.7 5.2 copy-start.1
  458.7 5.3 copy-start.24
  465.5 2.2 copy-start.25
  465.6 3.2 copy-start.28
  465.6 3.2 copy-start.46
  468.7 3.2 copy-start.45
  468.8 3.9 copy-start.27
  477.6 7.2 copy-start
  494.2 5.1 copy-start.1
  494.2 5.3 copy-start.24
  501.1 3.2 copy-start.28
  501.1 3.2 copy-start.46
  504.3 3.2 copy-start.45
  504.3 3.9 copy-start.27
  513.1 7.2 copy-start
  529.7 5.1 copy-start.1
  529.7 5.3 copy-start.24
  536.5 3.2 copy-start.28
  536.5 3.2 copy-start.46
  542.1 5.0 copy-start.12
  544.8 2.4 copy-start.19
  550.8 126.1 %reduce-scatter.15.cloned.1.call-start = ((), (), s32[]{:S(2)}) async-start(), calls=%async_computation.13 | async-start | bytes 2949120 | tf_op jit(solution)/shard_map/reduce_scatter | solution.py:112
  551.5 5.9 copy-start.43
  560.9 132.2 %reduce-scatter.25.cloned.1.call-start = ((), (), s32[]{:S(2)}) async-start(), calls=%async_computation.20 | async-start | bytes 2654208 | tf_op jit(solution)/shard_map/reduce_scatter | solution.py:197
  566.8 198.7 %reduce-scatter.23.cloned.1.call-start = ((), (), s32[]{:S(2)}) async-start(), calls=%async_computation.19 | async-start | bytes 2654208 | tf_op jit(solution)/shard_map/reduce_scatter | solution.py:195
  573.1 264.7 %reduce-scatter.21.cloned.1.call-start = ((), (), s32[]{:S(2)}) async-start(), calls=%async_computation.18 | async-start | bytes 2654208 | tf_op jit(solution)/shard_map/reduce_scatter | solution.py:192
  579.7 47.2 %copy-start.5 = (bf16[384,768]{1,0:T(8,128)(2,1)S(1)}, bf16[384,768]{1,0:T(8,128)(2,1)}, u32[]{:S(2)}) copy-start(bf16[384,768]{1,0:T(8,128)(2,1)} %param.19) | copy-start | bytes 1769476
  579.7 47.2 %copy-start.30 = (f32[384]{0:T(512)S(1)}, f32[384]{0:T(512)}, u32[]{:S(2)}) copy-start(f32[384]{0:T(512)} %copy-done.29) | copy-start | bytes 4612
  579.7 47.2 %copy-start.32 = (f32[768]{0:T(1024)S(1)}, f32[768]{0:T(1024)}, u32[]{:S(2)}) copy-start(f32[768]{0:T(1024)} %copy-done.31) | copy-start | bytes 9220
  579.7 50.0 %copy-start.35 = (f32[384]{0:T(512)S(1)}, f32[384]{0:T(512)}, u32[]{:S(2)}) copy-start(f32[384]{0:T(512)} %copy-done.34) | copy-start | bytes 4612
  579.8 52.4 %copy-start.8 = (f32[384,768]{1,0:T(8,128)S(1)}, f32[384,768]{1,0:T(8,128)}, u32[]{:S(2)}) copy-start(f32[384,768]{1,0:T(8,128)} %copy-done.7) | copy-start | bytes 3538948
  579.8 52.4 %copy-start.37 = (f32[384]{0:T(512)S(1)}, f32[384]{0:T(512)}, u32[]{:S(2)}) copy-start(f32[384]{0:T(512)} %copy-done.36) | copy-start | bytes 4612
  626.9 5.2 copy-start.9
  (17 other events, 22.0 us)
Sparse Core Ops, SparseCore 0:
  59.6 23.9 all-gather.6
  198.7 47.1 reduce-scatter.12
  401.6 24.0 all-gather.16
Sparse Core Ops, SparseCore 1:
  201.5 40.8 all-gather.10
  249.0 23.9 all-gather.8
  275.2 41.5 all-gather.12
  318.4 22.4 all-gather.14
  362.0 32.9 reduce-scatter.16
  429.6 62.5 reduce-scatter.26
  550.9 33.0 reduce-scatter.18
  586.3 33.0 reduce-scatter.14
  623.7 69.3 reduce-scatter.24
  697.6 67.9 reduce-scatter.22
  769.9 67.9 reduce-scatter.20
where the time goes:
time: 856 us; the launch traced here: 845 us
  waiting for transfers between devices  322 us (38%)
  blocking collectives  239 us (28%)
  matrix products  135 us (16%)
  other arithmetic  77.1 us (9%)
  local copies, waits for them, and re-layouts  43.6 us (5%)
  between operations  16.9 us (2%)
  loops' own time  10.2 us (1%)
    unnamed x3, blocking collectives  117 us
    dot_general x28, matrix products, contract(): return jnp.einsum(pattern, left, right, preferred_element_type=jnp.float32)  115 us
    reduce_scatter x1, waiting for transfers between devices, on_device(): lax.psum_scatter(grad_fc1, 'dp', scatter_dimension=0, tiled=True)  72.5 us
    reduce_scatter x1, waiting for transfers between devices, on_device(): lax.psum_scatter(grad_in_w, 'dp', scatter_dimension=0, tiled=True)  72.3 us
    reduce_scatter x1, waiting for transfers between devices, on_device(): lax.psum_scatter(attn_partial, 'tensor', scatter_dimension=0, tiled=True)  46.7 us
    all_gather x1, blocking collectives, on_device(): lax.all_gather(in_weight, 'dp', axis=0, tiled=True)  33.8 us
    all_gather x1, waiting for transfers between devices, on_device(): lax.all_gather(fc2_weight, 'dp', axis=1, tiled=True)  33.6 us
    reduce_scatter x1, waiting for transfers between devices, on_device(): lax.psum_scatter(contract('lf,df->ld', grad_hidden, fc1_full).astype(jnp....  33 us
  transfers between devices with their start and end apart: 14, of which 8 were waited for; matrix products, arithmetic and copies ran while one was open for 20% of the time, Pallas kernels for 0%

commit v1 on v0

--- a/solution.py
+++ b/solution.py
@@ -2,8 +2,35 @@
 import jax.numpy as jnp
 from jax import lax
 from jax.sharding import PartitionSpec as P
+from jax.lax import axis_index, axis_size, ppermute
 
 HD = 64
+
+
+def review_the_series_all(xx, out_dim):
+    xx = jnp.moveaxis(xx, 0, out_dim)
+    met_up = xx.shape
+    return xx.reshape(
+        *met_up[:out_dim], met_up[out_dim] * met_up[out_dim + 1], *met_up[out_dim + 2 :]
+    )
+
+
+def serve_records(k_dim, named_axis, frame_in):
+    n_all = axis_size(named_axis)
+    vals = tuple(((ix, (ix + 1) % n_all) for ix in range(n_all)))
+    steps_seen = tuple(((ii, h) for h, ii in vals))
+    step_out, w2 = ([], [])
+    for m in range(n_all - 1):
+        if m % 2 == 0:
+            step_out.append(
+                ppermute(step_out[-1] if step_out else frame_in, perm=vals, axis_name=named_axis)
+            )
+        else:
+            w2.append(ppermute(w2[-1] if w2 else frame_in, axis_name=named_axis, perm=steps_seen))
+    x_next = jnp.stack([*step_out[::-1], frame_in, *w2])
+    vec_out = axis_index(named_axis) - len(step_out)
+    x_next = x_next[(jnp.arange(n_all) - vec_out) % n_all]
+    return review_the_series_all(x_next, k_dim)
 
 
 def layer_norm(row_block, norm_gain, norm_shift):
@@ -47,7 +74,7 @@
         lax.all_gather(fc2_bias, ("dp", "tensor"), axis=0, tiled=True),
     )
     in_full, proj_full, out_full, fc1_full, fc1b_full, fc2_full = (
-        lax.all_gather(in_weight, "dp", axis=0, tiled=True),
+        serve_records(0, "dp", in_weight),
         lax.all_gather(proj_bias, "dp", axis=2, tiled=True),
         lax.all_gather(out_weight, "dp", axis=1, tiled=True),
         lax.all_gather(fc1_weight, "dp", axis=0, tiled=True),

time: 856 us -> 843 us (0.985)
  blocking collectives: 239 us -> 206 us
  starting transfers between devices: 0.98 us -> 15.9 us
    all_gather x1 -> x0, blocking collectives: 33.8 us -> none  [on_device(): lax.all_gather(in_weight, 'dp', axis=0, tiled=True)]
    ppermute x0 -> x7, starting transfers between devices: none -> 14.9 us  [the longest x3 11.6 us: serve_records(): ppermute(w2[-1] if w2 else frame_in, axis_name=named_axis, perm=steps_seen)]
    unnamed x100 -> x109, local copies, waits for them, and re-layouts: 20.8 us -> 23.9 us
  transfers between devices with their start and end apart: 14 -> 21, of which waited for: 8 -> 10; matrix products, arithmetic and copies ran while one was open for 20% -> 21% of each run, Pallas kernels for 0% -> 0%
where the time goes in v1:
time: 843 us; the launch traced here: 837 us
  waiting for transfers between devices  326 us (39%)
  blocking collectives  206 us (24%)
  matrix products  133 us (16%)
  other arithmetic  76.9 us (9%)
  local copies, waits for them, and re-layouts  51.2 us (6%)
  between operations  17.3 us (2%)
  starting transfers between devices  15.9 us (2%)
  loops' own time  10.2 us (1%)
    unnamed x3, blocking collectives  117 us
    dot_general x28, matrix products, contract(): return jnp.einsum(pattern, left, right, preferred_element_type=jnp.float32)  114 us
    reduce_scatter x1, waiting for transfers between devices, on_device(): lax.psum_scatter(grad_fc1, 'dp', scatter_dimension=0, tiled=True)  72.4 us
    reduce_scatter x1, waiting for transfers between devices, on_device(): lax.psum_scatter(grad_in_w, 'dp', scatter_dimension=0, tiled=True)  72.4 us
    reduce_scatter x1, waiting for transfers between devices, on_device(): lax.psum_scatter(attn_partial, 'tensor', scatter_dimension=0, tiled=True)  50 us
    all_gather x1, waiting for transfers between devices, on_device(): lax.all_gather(fc2_weight, 'dp', axis=1, tiled=True)  33.9 us
    reduce_scatter x1, waiting for transfers between devices, on_device(): lax.psum_scatter(contract('lf,df->ld', grad_hidden, fc1_full).astype(jnp....  33.1 us
    all_gather x1, blocking collectives, on_device(): lax.all_gather(out_weight, 'dp', axis=1, tiled=True)  32.3 us
  transfers between devices with their start and end apart: 21, of which 10 were waited for; matrix products, arithmetic and copies ran while one was open for 21% of the time, Pallas kernels for 0%

profile of v1, /device:TPU:0, one launch (start us, length us, event | category | flops | bytes accessed | tf_op | source)
XLA Modules:
  0.0 837.4 jit_solution(4911257499384798782)
XLA Ops:
  15.0 42.3 %all-reduce.15 = (f32[768]{0:T(1024)S(1)}, f32[768]{0:T(1024)S(1)}, f32[768]{0:T(1024)S(1)}, f32[768]{0:T(1024)S(1)}, f32[768]{0:T(1024)S(1)}) all-reduce(f32[768]{0:T(1024)S(1)} %dynamic-update-slice.1, f32[768]{0:T(1024)S(1)} %dynamic-update-slice, f32[768]{0:T(1024)S(1)} %dynamic-update-slice.2, ...), channel_id=1, replica_groups=mesh['dp'=8,'tensor'=4] {'dp','tensor'}, use_global_device_ids=true, to_apply=%add.1 | all-reduce | flops 3840 | bytes 30720
  57.3 2.2 fusion.49
  59.6 2.3 collective-permute-start
  61.9 2.4 collective-permute-start.4
  64.5 30.4 %all_gather.48 = bf16[2,3,64]{1,0,2:T(2,128)(2,1)S(1)} all-gather(bf16[2,3,8]{1,0,2:T(2,128)(2,1)S(1)} %copy.64), channel_id=1, replica_groups=mesh['dp'=8,'tensor'=4] {'dp'}, dimensions={2}, use_global_device_ids=true | all-gather | bytes 864 | tf_op jit(solution)/shard_map/all_gather | solution.py:78
  95.3 32.3 %all_gather.49 = bf16[192,768]{0,1:T(8,128)(2,1)S(1)} all-gather(bf16[192,96]{0,1:T(8,128)(2,1)S(1)} %copy.68), channel_id=1, replica_groups=mesh['dp'=8,'tensor'=4] {'dp'}, dimensions={1}, use_global_device_ids=true | all-gather | bytes 331776 | tf_op jit(solution)/shard_map/all_gather | solution.py:79
  128.6 3.9 collective-permute-start.5
  132.5 3.0 collective-permute-done.2
  135.5 5.3 collective-permute-start.6
  140.8 2.6 collective-permute-done.3
  146.6 3.2 fusion.38
  150.3 34.5 %while.27 = (s32[]{:T(128)}, bf16[3,512,192]{1,2,0:T(8,128)(2,1)}, f32[3,3,512]{2,1,0:T(4,128)}, s32[3]{0:T(128)S(1)}, s32[1536]{0:T(1024)S(1)}, /*index=5*/s32[...) while((s32[]{:T(128)}, bf16[3,512,192]{1,2,0:T(8,128)(2,1)}, ...), condition=%wide.region_5.6_spmd, body=%wide.region_2.5_spmd.sunk | while | flops 633174528 | bytes 33499348 | solution.py:126
  154.1 2.8 fusion.120
  156.9 3.5 fusion.121
  165.6 2.8 fusion.120
  168.4 3.5 fusion.121
  175.1 2.0 fusion.119
  177.1 2.8 fusion.120
  179.9 3.5 fusion.121
  186.1 3.0 fusion.68
  189.7 50.0 %reduce-scatter.13.cloned.1.call-done = f32[384,768]{1,0:T(8,128)} async-done(((f32[1536,768]{1,0:T(8,128)}), f32[384,768]{1,0:T(8,128)}) %reduce-scatter.13.cloned.1.call-update) | async-done | bytes 1179664 | tf_op jit(solution)/shard_map/reduce_scatter | solution.py:129
  244.0 26.2 %all_gather.55 = bf16[12,64]{0,1:T(8,128)(2,1)S(1)} all-gather(bf16[12,8]{0,1:T(8,128)(2,1)S(1)} %copy-done.42), channel_id=1, replica_groups=mesh['dp'=8,'tensor'=4] {'dp'}, dimensions={1}, use_global_device_ids=true | all-gather | bytes 1728 | tf_op jit(solution)/shard_map/all_gather | solution.py:81
  270.4 6.2 fusion.69
  276.6 33.9 %all-gather.13.cloned.1.call-done = bf16[768,768]{0,1:T(8,128)(2,1)} async-done(((bf16[768,96]{0,1:T(8,128)(2,1)}), bf16[768,768]{0,1:T(8,128)(2,1)}) %all-gather.13.cloned.1.call-update) | async-done | bytes 1179664 | tf_op jit(solution)/shard_map/all_gather | solution.py:82
  310.5 24.1 %all-gather.15.cloned.1.call-done = bf16[1536,768]{1,0:T(8,128)(2,1)} async-done(((bf16[384,768]{1,0:T(8,128)(2,1)}), bf16[1536,768]{1,0:T(8,128)(2,1)}) %all-gather.15.cloned.1.call-update) | async-done | bytes 2359312 | tf_op jit(solution)/shard_map/all_gather | solution.py:148
  334.6 16.1 %convert_reduce_fusion = (f32[768]{0:T(1024)}, bf16[1536,768]{1,0:T(8,128)(2,1)S(1)}, f32[1536,768]{1,0:T(8,128)}) fusion(f32[1536,768]{1,0:T(8,128)} %fusion.69, f32[768]{0:T(1024)S(1)} %reshape.273, bf16[1536,768]{1,0:T(8,128)(2,1)} %all-gather.15.cloned.1.call-done, bf16[768,768]{0,1:T(8,128)(2,1)} %all-gather.13.cloned.1.call-done), kind=kOutput, calls=%fused_computation.43 | convolution fusion | flops 1900412160 | bytes 15341568 | tf_op jit(solution)/shard_map/ld,fd->lf/dot_general | solution.py:48
  352.1 3.6 convolution_convert_fusion
  355.7 33.1 %reduce-scatter.17.cloned.1.call-done = bf16[384,768]{1,0:T(8,128)(2,1)} async-done(((bf16[1536,768]{1,0:T(8,128)(2,1)}), bf16[384,768]{1,0:T(8,128)(2,1)}) %reduce-scatter.17.cloned.1.call-update) | async-done | bytes 589840 | tf_op jit(solution)/shard_map/reduce_scatter | solution.py:154
  388.8 2.2 fusion.53
  395.4 2.9 reshape.270
  398.3 21.2 %all-gather.17.cloned.1.call-done = bf16[1536,768]{1,0:T(8,128)(2,1)} async-done(((bf16[384,768]{1,0:T(8,128)(2,1)}), bf16[1536,768]{1,0:T(8,128)(2,1)}) %all-gather.17.cloned.1.call-update) | async-done | bytes 2359312 | tf_op jit(solution)/shard_map/all_gather | solution.py:166
  419.5 3.8 convolution_bitcast_fusion
  423.6 3.5 convolution_convert_fusion.2
  427.0 106.5 %while.28 = (s32[]{:T(128)}, f32[1536,3,64]{0,2,1:T(8,128)}, f32[1536,3,64]{0,2,1:T(8,128)S(1)}, bf16[3,512,3,64]{1,3,2,0:T(8,128)(2,1)}, s32[3]{0:T(128)S(1)}, ...) while((s32[]{:T(128)}, f32[1536,3,64]{0,2,1:T(8,128)}, ...), condition=%wide.region_15.16_spmd.clone, body=%wide.region_13.15_spmd.clone.sunk | while | flops 1533540864 | bytes 150903440 | solution.py:193
  433.5 2.4 fusion.131
  435.9 7.2 multiply_reduce_fusion.3
  443.1 9.4 %multiply_convert_fusion.3 = bf16[3,512,1536]{2,1,0:T(8,128)(2,1)} fusion(f32[3,512,1536]{2,1,0:T(8,128)} %get-tuple-element.446, f32[3,512,1536]{2,1,0:T(8,128)} %copy-done, f32[3,512]{1,0:T(4,128)S(1)} %get-tuple-element.447), kind=kLoop, calls=%fused_computation.16.clone.1 | loop fusion | flops 7077888 | bytes 23599104 | tf_op jit(solution)/shard_map/while/body/eval_jaxpr/convert_element_type | solution.py:184
  452.5 5.0 fusion.133
  459.4 2.1 fusion.132
  469.1 2.4 fusion.131
  471.4 7.2 multiply_reduce_fusion.3
  478.6 9.4 %multiply_convert_fusion.3 = bf16[3,512,1536]{2,1,0:T(8,128)(2,1)} fusion(f32[3,512,1536]{2,1,0:T(8,128)} %get-tuple-element.446, f32[3,512,1536]{2,1,0:T(8,128)} %copy-done, f32[3,512]{1,0:T(4,128)S(1)} %get-tuple-element.447), kind=kLoop, calls=%fused_computation.16.clone.1 | loop fusion | flops 7077888 | bytes 23599104 | tf_op jit(solution)/shard_map/while/body/eval_jaxpr/convert_element_type | solution.py:184
  488.1 5.0 fusion.133
  494.9 2.1 fusion.132
  504.6 2.4 fusion.131
  506.9 7.2 multiply_reduce_fusion.3
  514.2 9.4 %multiply_convert_fusion.3 = bf16[3,512,1536]{2,1,0:T(8,128)(2,1)} fusion(f32[3,512,1536]{2,1,0:T(8,128)} %get-tuple-element.446, f32[3,512,1536]{2,1,0:T(8,128)} %copy-done, f32[3,512]{1,0:T(4,128)S(1)} %get-tuple-element.447), kind=kLoop, calls=%fused_computation.16.clone.1 | loop fusion | flops 7077888 | bytes 23599104 | tf_op jit(solution)/shard_map/while/body/eval_jaxpr/convert_element_type | solution.py:184
  523.5 5.0 fusion.133
  530.4 2.1 fusion.132
  539.1 3.6 bitcast_convert_fusion
  543.4 4.5 multiply_convert_fusion.1
  548.0 3.5 convolution_convert_fusion.1
  551.5 5.2 fusion.71
  558.4 5.2 fusion.70
  565.0 5.2 fusion.36
  579.3 37.0 %all-reduce.16 = (f32[2,3,64]{2,1,0:T(4,128)}, f32[12,64]{1,0:T(8,128)}) all-reduce(f32[2,3,64]{2,1,0:T(4,128)} %reshape.271, f32[12,64]{1,0:T(8,128)} %reshape.272), channel_id=9, replica_groups=mesh['dp'=8,'tensor'=4] {'dp'}, use_global_device_ids=true, to_apply=%region_25.26.clone | all-reduce | flops 1152 | bytes 9216
  622.1 2.2 convert_reduce_fusion.2
  625.0 2.4 fusion.54
  627.4 2.2 add_add_fusion.2
  629.6 37.8 %all-reduce.14 = (f32[768]{0:T(1024)S(1)}, f32[768]{0:T(1024)S(1)}, f32[768]{0:T(1024)S(1)}, f32[768]{0:T(1024)S(1)}, f32[768]{0:T(1024)S(1)}, /*index=5*/f32[768]{0:T(1024)S(1)}, f32[768]{0:T(1024)S(1)}) all-reduce(f32[768]{0:T(1024)} %dynamic-update-slice.5, ...), channel_id=1, replica_groups=mesh['dp'=8,'tensor'=4] {'dp','tensor'}, use_global_device_ids=true, to_apply=%add.5 | all-reduce | flops 5376 | bytes 43008
  670.9 2.0 add_convert_fusion.1
  673.0 11.9 %reduce-scatter.25.cloned.1.call-done = f32[768,96]{0,1:T(8,128)} async-done(((f32[768,768]{0,1:T(8,128)}), f32[768,96]{0,1:T(8,128)}) %reduce-scatter.25.cloned.1.call-update) | async-done | bytes 294928 | tf_op jit(solution)/shard_map/reduce_scatter | solution.py:224
  684.9 72.4 %reduce-scatter.23.cloned.1.call-done = f32[96,768]{1,0:T(8,128)} async-done(((f32[768,768]{1,0:T(8,128)}), f32[96,768]{1,0:T(8,128)}) %reduce-scatter.23.cloned.1.call-update) | async-done | bytes 294928 | tf_op jit(solution)/shard_map/reduce_scatter | solution.py:222
  757.3 72.4 %reduce-scatter.21.cloned.1.call-done = f32[96,3,192]{2,0,1:T(8,128)} async-done(((f32[768,3,192]{2,0,1:T(8,128)}), f32[96,3,192]{2,0,1:T(8,128)}) %reduce-scatter.21.cloned.1.call-update) | async-done | bytes 221200 | tf_op jit(solution)/shard_map/reduce_scatter | solution.py:219
  (296 shorter events, 83.6 us)
Async XLA Ops:
  8.0 51.6 %copy-start.27 = (bf16[96,3,192]{2,0,1:T(8,128)(2,1)S(1)}, bf16[96,3,192]{2,0,1:T(8,128)(2,1)}, u32[]{:S(2)}) copy-start(bf16[96,3,192]{2,0,1:T(8,128)(2,1)} %param.23) | copy-start | bytes 331780
  8.0 56.3 %copy-start.43 = (bf16[2,3,8]{2,0,1:T(2,128)(2,1)S(1)}, bf16[2,3,8]{2,0,1:T(2,128)(2,1)}, u32[]{:S(2)}) copy-start(bf16[2,3,8]{2,0,1:T(2,128)(2,1)} %param.24) | copy-start | bytes 292
  8.0 86.9 %copy-start.24 = (s32[1,1536]{1,0:T(1,128)S(1)}, s32[1,1536]{1,0:T(1,128)}, u32[]{:S(2)}) copy-start(s32[1,1536]{1,0:T(1,128)} %param.20) | copy-start | bytes 18436
  8.0 87.1 %copy-start.34 = (bf16[192,96]{1,0:T(8,128)(2,1)S(1)}, bf16[192,96]{1,0:T(8,128)(2,1)}, u32[]{:S(2)}) copy-start(bf16[192,96]{1,0:T(8,128)(2,1)} %param.25) | copy-start | bytes 110596
  8.1 138.5 %all-gather.7.cloned.1.call-start = ((), (), s32[]{:S(2)}) async-start(), calls=%async_computation.8 | async-start | bytes 2949120 | tf_op jit(solution)/shard_map/all_gather | solution.py:93
  9.4 55.0 %copy-start.30 = (f32[384]{0:T(512)}, f32[384]{0:T(512)S(1)}, u32[]{:S(2)}) copy-start(f32[384]{0:T(512)S(1)} %broadcast_multiply_fusion.1) | copy-start | bytes 4612
  10.7 3.4 copy-start.39
  10.8 53.6 %copy-start.35 = (f32[384]{0:T(512)}, f32[384]{0:T(512)S(1)}, u32[]{:S(2)}) copy-start(f32[384]{0:T(512)S(1)} %fusion.57) | copy-start | bytes 4612
  57.3 7.0 copy-start.32
  59.5 180.2 %reduce-scatter.13.cloned.1.call-start = ((), (), s32[]{:S(2)}) async-start(), calls=%async_computation.9 | async-start | bytes 5898240 | tf_op jit(solution)/shard_map/reduce_scatter | solution.py:129
  59.6 35.7 %collective-permute-start = (bf16[96,3,192]{2,0,1:T(8,128)(2,1)S(1)}, bf16[96,3,192]{2,0,1:T(8,128)(2,1)S(1)}, u32[]{:S(2)}, u32[]{:S(2)}) collective-permute-start(bf16[96,3,192]{2,0,1:T(8,128)(2,1)S(1)} %copy-done.27), channel_id=1, source_target_pairs={{0,4},{4,8},{8,12},{12,16},{16,20},{20,24},{24,28},{28,0},{1,5},{5... | collective-permute-start | bytes 331784 | tf_op jit(solution)/shard_map/ppermute | solution.py:26
  61.9 66.7 %collective-permute-start.4 = (bf16[96,3,192]{2,0,1:T(8,128)(2,1)S(1)}, bf16[96,3,192]{2,0,1:T(8,128)(2,1)S(1)}, u32[]{:S(2)}, u32[]{:S(2)}) collective-permute-start(bf16[96,3,192]{2,0,1:T(8,128)(2,1)S(1)} %copy-done.27), channel_id=1, source_target_pairs={{4,0},{8,4},{12,8},{16,12},{20,16},{24,20},{28,24},{0,28},{5,1},{9... | collective-permute-start | bytes 331784 | tf_op jit(solution)/shard_map/ppermute | solution.py:29
  95.3 32.4 %collective-permute-start.1 = (bf16[96,3,192]{2,0,1:T(8,128)(2,1)S(1)}, bf16[96,3,192]{2,0,1:T(8,128)(2,1)S(1)}, u32[]{:S(2)}, u32[]{:S(2)}) collective-permute-start(bf16[96,3,192]{2,0,1:T(8,128)(2,1)S(1)} %collective-permute-done), channel_id=1, source_target_pairs={{0,4},{4,8},{8,12},{12,16},{16,20},{20,24},{24,28},{28,0},{1,5},{5... | collective-permute-start | bytes 331784 | tf_op jit(solution)/shard_map/ppermute | solution.py:26
  127.7 58.5 %copy-start.13 = (bf16[192,768]{0,1:T(8,128)(2,1)}, bf16[192,768]{0,1:T(8,128)(2,1)S(1)}, u32[]{:S(2)}) copy-start(bf16[192,768]{0,1:T(8,128)(2,1)S(1)} %all_gather.49) | copy-start | bytes 884740
  127.7 7.8 collective-permute-start.2
  128.6 6.9 collective-permute-start.5
  135.5 7.8 collective-permute-start.3
  135.5 8.0 collective-permute-start.6
  145.6 4.2 copy-start.9
  184.8 4.3 copy-start.6
  189.1 50.6 %copy-start.4 = (bf16[384,768]{1,0:T(8,128)(2,1)S(1)}, bf16[384,768]{1,0:T(8,128)(2,1)}, u32[]{:S(2)}) copy-start(bf16[384,768]{1,0:T(8,128)(2,1)} %param.19) | copy-start | bytes 1769476
  189.1 81.3 %all-gather.11.cloned.1.call-start = ((), (), s32[]{:S(2)}) async-start(), calls=%async_computation.11 | async-start | bytes 1327104 | tf_op jit(solution)/shard_map/all_gather | solution.py:80
  189.7 80.7 %all-gather.9.cloned.1.call-start = ((), (), s32[]{:S(2)}) async-start(), calls=%async_computation.10 | async-start | bytes 2949120 | tf_op jit(solution)/shard_map/all_gather | solution.py:133
  242.6 67.9 %all-gather.13.cloned.1.call-start = ((), (), s32[]{:S(2)}) async-start(), calls=%async_computation.12 | async-start | bytes 1327104 | tf_op jit(solution)/shard_map/all_gather | solution.py:82
  243.2 91.4 %all-gather.15.cloned.1.call-start = ((), (), s32[]{:S(2)}) async-start(), calls=%async_computation.14 | async-start | bytes 2949120 | tf_op jit(solution)/shard_map/all_gather | solution.py:148
  243.9 144.9 %reduce-scatter.17.cloned.1.call-start = ((), (), s32[]{:S(2)}) async-start(), calls=%async_computation.15 | async-start | bytes 2949120 | tf_op jit(solution)/shard_map/reduce_scatter | solution.py:154
  270.4 64.2 %copy-start.40 = (f32[768]{0:T(1024)}, f32[768]{0:T(1024)S(1)}, u32[]{:S(2)}) copy-start(f32[768]{0:T(1024)S(1)} %reshape.273) | copy-start | bytes 9220
  334.6 17.5 %copy-start.45 = (bf16[768,768]{1,0:T(8,128)(2,1)S(1)}, bf16[768,768]{1,0:T(8,128)(2,1)}, u32[]{:S(2)}) copy-start(bf16[768,768]{1,0:T(8,128)(2,1)} %all-gather.11.cloned.1.call-done) | copy-start | bytes 3538948
  355.7 37.9 %copy-start.11 = (bf16[384,768]{1,0:T(8,128)(2,1)S(1)}, bf16[384,768]{1,0:T(8,128)(2,1)}, u32[]{:S(2)}) copy-start(bf16[384,768]{1,0:T(8,128)(2,1)} %param.33) | copy-start | bytes 1769476
  355.7 63.8 %all-gather.17.cloned.1.call-start = ((), (), s32[]{:S(2)}) async-start(), calls=%async_computation.16 | async-start | bytes 2949120 | tf_op jit(solution)/shard_map/all_gather | solution.py:166
  395.3 225.1 %reduce-scatter.27.cloned.1.call-start = ((), (), s32[]{:S(2)}) async-start(), calls=%async_computation.21 | async-start | bytes 884736
  423.3 198.8 %reduce-scatter.19.cloned.1.call-start = ((), (), s32[]{:S(2)}) async-start(), calls=%async_computation.17 | async-start | bytes 2949120 | tf_op jit(solution)/shard_map/reduce_scatter | solution.py:209
  427.0 3.8 copy-start.28
  435.8 7.2 copy-start
  452.5 5.2 copy-start.1
  452.5 5.3 copy-start.25
  459.4 3.2 copy-start.29
  459.4 3.2 copy-start.47
  462.6 3.2 copy-start.46
  462.6 3.9 copy-start.28
  471.4 7.2 copy-start
  488.1 5.1 copy-start.1
  488.1 5.3 copy-start.25
  494.9 3.2 copy-start.29
  498.1 3.2 copy-start.46
  498.1 3.9 copy-start.28
  506.9 7.2 copy-start
  523.5 5.1 copy-start.1
  523.5 5.3 copy-start.25
  530.3 3.2 copy-start.29
  530.4 3.2 copy-start.47
  542.8 128.2 %reduce-scatter.15.cloned.1.call-start = ((), (), s32[]{:S(2)}) async-start(), calls=%async_computation.13 | async-start | bytes 2949120 | tf_op jit(solution)/shard_map/reduce_scatter | solution.py:139
  543.4 4.5 copy-start.44
  551.5 133.4 %reduce-scatter.25.cloned.1.call-start = ((), (), s32[]{:S(2)}) async-start(), calls=%async_computation.20 | async-start | bytes 2654208 | tf_op jit(solution)/shard_map/reduce_scatter | solution.py:224
  556.8 200.5 %reduce-scatter.23.cloned.1.call-start = ((), (), s32[]{:S(2)}) async-start(), calls=%async_computation.19 | async-start | bytes 2654208 | tf_op jit(solution)/shard_map/reduce_scatter | solution.py:222
  563.6 266.0 %reduce-scatter.21.cloned.1.call-start = ((), (), s32[]{:S(2)}) async-start(), calls=%async_computation.18 | async-start | bytes 2654208 | tf_op jit(solution)/shard_map/reduce_scatter | solution.py:219
  570.2 51.9 %copy-start.5 = (bf16[384,768]{1,0:T(8,128)(2,1)S(1)}, bf16[384,768]{1,0:T(8,128)(2,1)}, u32[]{:S(2)}) copy-start(bf16[384,768]{1,0:T(8,128)(2,1)} %param.19) | copy-start | bytes 1769476
  570.2 51.9 %copy-start.31 = (f32[384]{0:T(512)S(1)}, f32[384]{0:T(512)}, u32[]{:S(2)}) copy-start(f32[384]{0:T(512)} %copy-done.30) | copy-start | bytes 4612
  570.2 51.9 %copy-start.33 = (f32[768]{0:T(1024)S(1)}, f32[768]{0:T(1024)}, u32[]{:S(2)}) copy-start(f32[768]{0:T(1024)} %copy-done.32) | copy-start | bytes 9220
  570.2 54.8 %copy-start.36 = (f32[384]{0:T(512)S(1)}, f32[384]{0:T(512)}, u32[]{:S(2)}) copy-start(f32[384]{0:T(512)} %copy-done.35) | copy-start | bytes 4612
  570.2 57.2 %copy-start.8 = (f32[384,768]{1,0:T(8,128)S(1)}, f32[384,768]{1,0:T(8,128)}, u32[]{:S(2)}) copy-start(f32[384,768]{1,0:T(8,128)} %copy-done.7) | copy-start | bytes 3538948
  570.2 57.2 %copy-start.12 = (bf16[384,768]{1,0:T(8,128)(2,1)S(1)}, bf16[384,768]{1,0:T(8,128)(2,1)}, u32[]{:S(2)}) copy-start(bf16[384,768]{1,0:T(8,128)(2,1)} %param.33) | copy-start | bytes 1769476
  570.2 57.1 %copy-start.38 = (f32[384]{0:T(512)S(1)}, f32[384]{0:T(512)}, u32[]{:S(2)}) copy-start(f32[384]{0:T(512)} %copy-done.37) | copy-start | bytes 4612
  622.1 5.3 copy-start.10
  (25 other events, 44.5 us)
Sparse Core Ops, SparseCore 0:
  59.6 23.9 all-gather.6
  189.2 50.4 reduce-scatter.12
  395.4 24.0 all-gather.16
Sparse Core Ops, SparseCore 1:
  192.0 44.1 all-gather.10
  242.7 23.9 all-gather.8
  268.9 41.5 all-gather.12
  312.1 22.4 all-gather.14
  355.8 33.0 reduce-scatter.16
  423.4 62.5 reduce-scatter.26
  542.9 32.9 reduce-scatter.18
  578.3 33.0 reduce-scatter.14
  615.6 69.2 reduce-scatter.24
  689.4 67.9 reduce-scatter.22
  761.6 68.0 reduce-scatter.20
